TPU v7x, 256 devices: a whole 4x4x8 slice. The times are simulated.
256 devices in a mesh: rows: 16 (over z, core), feat: 16 (over x, y).
Axes of the slice: x: 4, y: 4, z: 8, core: 2. Of those that a mesh axis runs over, the one named last changes fastest.
Arguments:
- features: bfloat16 [16384, 16384], P('rows', 'feat'), may hold values from -0.046875 to 0.046875
- inverse_gram: float32 [16384, 1024], P('feat'), as said below
- targets: float32 [128, 16384], P('feat', 'rows'), may hold values from -6 to 6
Outputs:
- weights: float32 [128, 16384], P(None, 'feat')
- residual: float32 [128, 16384], P('feat', 'rows')
Inputs may be any that keep to these rules, and one draw needn't show every extreme that they name: Each block of inverse_gram is symmetric.
All inputs are finite; a program needn't handle non-finite values.
Results may differ from a plain program's by a relative error of at most 0.007.
Values sent between devices are 32-bit elements; how exact they have to be, the bound alone decides.
No kernel may reach another device: no remote copies, remote signals or barrier semaphores. Data moves between devices by JAX's collectives and lax.ppermute only.
A program may use at most 64 MiB of HBM per device.

v0:
```python
import jax
import jax.numpy as jnp
from jax import lax
from jax.sharding import PartitionSpec as P

TGT = 128
TURNS = 2
ridge_weight = 0.5


def passed_along(block, axis, distance):
    devices = range(lax.axis_size(axis))
    route = [((i - distance) % len(devices), i) for i in devices]
    return lax.ppermute(block, axis, route)


def local(features, inverse_gram, targets):
    block_count = lax.axis_size("feat")
    position = lax.axis_index("feat")
    panel_width = targets.shape[0]

    def refine(panel_rows, panel_weights):
        partial_value = jnp.dot(
            panel_rows.astype(jnp.bfloat16), features, preferred_element_type=jnp.float32
        )
        projection = lax.psum(partial_value, "rows")
        increment = jnp.dot(
            projection - ridge_weight * panel_weights, inverse_gram, precision=lax.Precision.HIGHEST
        )
        fitted = lax.dot_general(
            increment.astype(jnp.bfloat16),
            features,
            (((1,), (1,)), ((), ())),
            preferred_element_type=jnp.float32,
        )
        return (panel_rows - fitted, panel_weights + increment)

    def advance(section, carried):
        residual, weights = carried
        panel_index = (position - section) % block_count
        start = panel_index * panel_width
        panel_weights = lax.dynamic_slice_in_dim(weights, start, panel_width, 0)
        residual, panel_weights = refine(residual, panel_weights)
        weights = lax.dynamic_update_slice_in_dim(weights, panel_weights, start, 0)
        residual = passed_along(residual, "feat", 1)
        return (residual, weights)

    carried = (targets, jnp.zeros((TGT, features.shape[1]), jnp.float32))
    for sweep_index in range(TURNS):
        offset = sweep_index * block_count

        def sweep_step(inner, state, offset=offset):
            return advance(inner + offset, state)

        carried = lax.fori_loop(0, block_count, sweep_step, carried)
    residual, weights = carried
    return (weights, residual)


def solution(mesh):
    placed = (P("rows", "feat"), P("feat", None), P("feat", "rows"))
    return jax.shard_map(
        local,
        mesh=mesh,
        in_specs=placed,
        out_specs=(P(None, "feat"), P("feat", "rows")),
        check_vma=False,
    )
```

profile of v0, /device:TPU:0, one launch (start us, length us, event | category | flops | bytes accessed | tf_op | source)
XLA Modules:
  0.0 1925.4 jit_solution(16532286769631520528)
XLA Ops:
  1.4 963.3 %while.34 = (s32[]{:T(128)}, f32[8,1024]{1,0:T(8,128)S(1)}, f32[128,1024]{1,0:T(8,128)S(1)}, bf16[1024,1024]{1,0:T(8,128)(2,1)}, s32[]{:T(128)}, /*index=5*/f32[...) while((s32[]{:T(128)}, f32[8,1024]{1,0:T(8,128)S(1)}, ...), condition=%wide.region_2.3_spmd, body=%wide.region_0.2_spmd.sunk | while | flops 134275072 | bytes 17334632 | solution.py:55
  3.4 49.1 %psum.30 = f32[8,1024]{1,0:T(8,128)S(1)} all-reduce(f32[8,1024]{1,0:T(8,128)S(1)} %fusion.48), channel_id=1, replica_groups=mesh['rows'=16,'feat'=16] {'rows'}, use_global_device_ids=true, to_apply=%region_1.1 | all-reduce | flops 8192 | bytes 65536 | tf_op jit(solution)/shard_map/while/body/eval_jaxpr/psum | solution.py:26
  66.9 45.7 %psum.30 = f32[8,1024]{1,0:T(8,128)S(1)} all-reduce(f32[8,1024]{1,0:T(8,128)S(1)} %fusion.48), channel_id=1, replica_groups=mesh['rows'=16,'feat'=16] {'rows'}, use_global_device_ids=true, to_apply=%region_1.1 | all-reduce | flops 8192 | bytes 65536 | tf_op jit(solution)/shard_map/while/body/eval_jaxpr/psum | solution.py:26
  117.7 7.2 collective-permute-done
  126.9 45.7 %psum.30 = f32[8,1024]{1,0:T(8,128)S(1)} all-reduce(f32[8,1024]{1,0:T(8,128)S(1)} %fusion.48), channel_id=1, replica_groups=mesh['rows'=16,'feat'=16] {'rows'}, use_global_device_ids=true, to_apply=%region_1.1 | all-reduce | flops 8192 | bytes 65536 | tf_op jit(solution)/shard_map/while/body/eval_jaxpr/psum | solution.py:26
  177.7 7.2 collective-permute-done
  186.9 45.7 %psum.30 = f32[8,1024]{1,0:T(8,128)S(1)} all-reduce(f32[8,1024]{1,0:T(8,128)S(1)} %fusion.48), channel_id=1, replica_groups=mesh['rows'=16,'feat'=16] {'rows'}, use_global_device_ids=true, to_apply=%region_1.1 | all-reduce | flops 8192 | bytes 65536 | tf_op jit(solution)/shard_map/while/body/eval_jaxpr/psum | solution.py:26
  237.7 7.2 collective-permute-done
  246.9 45.7 %psum.30 = f32[8,1024]{1,0:T(8,128)S(1)} all-reduce(f32[8,1024]{1,0:T(8,128)S(1)} %fusion.48), channel_id=1, replica_groups=mesh['rows'=16,'feat'=16] {'rows'}, use_global_device_ids=true, to_apply=%region_1.1 | all-reduce | flops 8192 | bytes 65536 | tf_op jit(solution)/shard_map/while/body/eval_jaxpr/psum | solution.py:26
  297.7 7.2 collective-permute-done
  306.8 45.7 %psum.30 = f32[8,1024]{1,0:T(8,128)S(1)} all-reduce(f32[8,1024]{1,0:T(8,128)S(1)} %fusion.48), channel_id=1, replica_groups=mesh['rows'=16,'feat'=16] {'rows'}, use_global_device_ids=true, to_apply=%region_1.1 | all-reduce | flops 8192 | bytes 65536 | tf_op jit(solution)/shard_map/while/body/eval_jaxpr/psum | solution.py:26
  357.6 7.2 collective-permute-done
  366.8 45.7 %psum.30 = f32[8,1024]{1,0:T(8,128)S(1)} all-reduce(f32[8,1024]{1,0:T(8,128)S(1)} %fusion.48), channel_id=1, replica_groups=mesh['rows'=16,'feat'=16] {'rows'}, use_global_device_ids=true, to_apply=%region_1.1 | all-reduce | flops 8192 | bytes 65536 | tf_op jit(solution)/shard_map/while/body/eval_jaxpr/psum | solution.py:26
  417.6 7.2 collective-permute-done
  426.8 45.7 %psum.30 = f32[8,1024]{1,0:T(8,128)S(1)} all-reduce(f32[8,1024]{1,0:T(8,128)S(1)} %fusion.48), channel_id=1, replica_groups=mesh['rows'=16,'feat'=16] {'rows'}, use_global_device_ids=true, to_apply=%region_1.1 | all-reduce | flops 8192 | bytes 65536 | tf_op jit(solution)/shard_map/while/body/eval_jaxpr/psum | solution.py:26
  477.6 7.2 collective-permute-done
  486.8 45.7 %psum.30 = f32[8,1024]{1,0:T(8,128)S(1)} all-reduce(f32[8,1024]{1,0:T(8,128)S(1)} %fusion.48), channel_id=1, replica_groups=mesh['rows'=16,'feat'=16] {'rows'}, use_global_device_ids=true, to_apply=%region_1.1 | all-reduce | flops 8192 | bytes 65536 | tf_op jit(solution)/shard_map/while/body/eval_jaxpr/psum | solution.py:26
  537.6 7.2 collective-permute-done
  546.8 45.7 %psum.30 = f32[8,1024]{1,0:T(8,128)S(1)} all-reduce(f32[8,1024]{1,0:T(8,128)S(1)} %fusion.48), channel_id=1, replica_groups=mesh['rows'=16,'feat'=16] {'rows'}, use_global_device_ids=true, to_apply=%region_1.1 | all-reduce | flops 8192 | bytes 65536 | tf_op jit(solution)/shard_map/while/body/eval_jaxpr/psum | solution.py:26
  597.6 7.2 collective-permute-done
  606.8 45.7 %psum.30 = f32[8,1024]{1,0:T(8,128)S(1)} all-reduce(f32[8,1024]{1,0:T(8,128)S(1)} %fusion.48), channel_id=1, replica_groups=mesh['rows'=16,'feat'=16] {'rows'}, use_global_device_ids=true, to_apply=%region_1.1 | all-reduce | flops 8192 | bytes 65536 | tf_op jit(solution)/shard_map/while/body/eval_jaxpr/psum | solution.py:26
  657.6 7.2 collective-permute-done
  666.8 45.7 %psum.30 = f32[8,1024]{1,0:T(8,128)S(1)} all-reduce(f32[8,1024]{1,0:T(8,128)S(1)} %fusion.48), channel_id=1, replica_groups=mesh['rows'=16,'feat'=16] {'rows'}, use_global_device_ids=true, to_apply=%region_1.1 | all-reduce | flops 8192 | bytes 65536 | tf_op jit(solution)/shard_map/while/body/eval_jaxpr/psum | solution.py:26
  717.6 7.2 collective-permute-done
  726.8 45.7 %psum.30 = f32[8,1024]{1,0:T(8,128)S(1)} all-reduce(f32[8,1024]{1,0:T(8,128)S(1)} %fusion.48), channel_id=1, replica_groups=mesh['rows'=16,'feat'=16] {'rows'}, use_global_device_ids=true, to_apply=%region_1.1 | all-reduce | flops 8192 | bytes 65536 | tf_op jit(solution)/shard_map/while/body/eval_jaxpr/psum | solution.py:26
  777.6 7.2 collective-permute-done
  786.8 45.7 %psum.30 = f32[8,1024]{1,0:T(8,128)S(1)} all-reduce(f32[8,1024]{1,0:T(8,128)S(1)} %fusion.48), channel_id=1, replica_groups=mesh['rows'=16,'feat'=16] {'rows'}, use_global_device_ids=true, to_apply=%region_1.1 | all-reduce | flops 8192 | bytes 65536 | tf_op jit(solution)/shard_map/while/body/eval_jaxpr/psum | solution.py:26
  837.6 7.2 collective-permute-done
  846.7 45.7 %psum.30 = f32[8,1024]{1,0:T(8,128)S(1)} all-reduce(f32[8,1024]{1,0:T(8,128)S(1)} %fusion.48), channel_id=1, replica_groups=mesh['rows'=16,'feat'=16] {'rows'}, use_global_device_ids=true, to_apply=%region_1.1 | all-reduce | flops 8192 | bytes 65536 | tf_op jit(solution)/shard_map/while/body/eval_jaxpr/psum | solution.py:26
  897.5 7.2 collective-permute-done
  906.7 45.7 %psum.30 = f32[8,1024]{1,0:T(8,128)S(1)} all-reduce(f32[8,1024]{1,0:T(8,128)S(1)} %fusion.48), channel_id=1, replica_groups=mesh['rows'=16,'feat'=16] {'rows'}, use_global_device_ids=true, to_apply=%region_1.1 | all-reduce | flops 8192 | bytes 65536 | tf_op jit(solution)/shard_map/while/body/eval_jaxpr/psum | solution.py:26
  957.5 7.2 collective-permute-done
  964.8 959.8 %while.35 = (s32[]{:T(128)}, f32[8,1024]{1,0:T(8,128)S(1)}, f32[128,1024]{1,0:T(8,128)S(1)}, bf16[1024,1024]{1,0:T(8,128)(2,1)}, s32[]{:T(128)}, /*index=5*/f32[...) while((s32[]{:T(128)}, f32[8,1024]{1,0:T(8,128)S(1)}, ...), condition=%wide.region_5.6_spmd, body=%wide.region_3.5_spmd.sunk | while | flops 134275072 | bytes 17334644 | solution.py:55
  966.7 45.7 %psum.31 = f32[8,1024]{1,0:T(8,128)S(1)} all-reduce(f32[8,1024]{1,0:T(8,128)S(1)} %fusion.56), channel_id=1, replica_groups=mesh['rows'=16,'feat'=16] {'rows'}, use_global_device_ids=true, to_apply=%region_4.4 | all-reduce | flops 8192 | bytes 65536 | tf_op jit(solution)/shard_map/while/body/eval_jaxpr/psum | solution.py:26
  1017.5 7.2 collective-permute-done.1
  1026.7 45.7 %psum.31 = f32[8,1024]{1,0:T(8,128)S(1)} all-reduce(f32[8,1024]{1,0:T(8,128)S(1)} %fusion.56), channel_id=1, replica_groups=mesh['rows'=16,'feat'=16] {'rows'}, use_global_device_ids=true, to_apply=%region_4.4 | all-reduce | flops 8192 | bytes 65536 | tf_op jit(solution)/shard_map/while/body/eval_jaxpr/psum | solution.py:26
  1077.5 7.2 collective-permute-done.1
  1086.7 45.7 %psum.31 = f32[8,1024]{1,0:T(8,128)S(1)} all-reduce(f32[8,1024]{1,0:T(8,128)S(1)} %fusion.56), channel_id=1, replica_groups=mesh['rows'=16,'feat'=16] {'rows'}, use_global_device_ids=true, to_apply=%region_4.4 | all-reduce | flops 8192 | bytes 65536 | tf_op jit(solution)/shard_map/while/body/eval_jaxpr/psum | solution.py:26
  1137.5 7.2 collective-permute-done.1
  1146.7 45.7 %psum.31 = f32[8,1024]{1,0:T(8,128)S(1)} all-reduce(f32[8,1024]{1,0:T(8,128)S(1)} %fusion.56), channel_id=1, replica_groups=mesh['rows'=16,'feat'=16] {'rows'}, use_global_device_ids=true, to_apply=%region_4.4 | all-reduce | flops 8192 | bytes 65536 | tf_op jit(solution)/shard_map/while/body/eval_jaxpr/psum | solution.py:26
  1197.5 7.2 collective-permute-done.1
  1206.7 45.7 %psum.31 = f32[8,1024]{1,0:T(8,128)S(1)} all-reduce(f32[8,1024]{1,0:T(8,128)S(1)} %fusion.56), channel_id=1, replica_groups=mesh['rows'=16,'feat'=16] {'rows'}, use_global_device_ids=true, to_apply=%region_4.4 | all-reduce | flops 8192 | bytes 65536 | tf_op jit(solution)/shard_map/while/body/eval_jaxpr/psum | solution.py:26
  1257.5 7.2 collective-permute-done.1
  1266.7 45.7 %psum.31 = f32[8,1024]{1,0:T(8,128)S(1)} all-reduce(f32[8,1024]{1,0:T(8,128)S(1)} %fusion.56), channel_id=1, replica_groups=mesh['rows'=16,'feat'=16] {'rows'}, use_global_device_ids=true, to_apply=%region_4.4 | all-reduce | flops 8192 | bytes 65536 | tf_op jit(solution)/shard_map/while/body/eval_jaxpr/psum | solution.py:26
  1317.5 7.2 collective-permute-done.1
  1326.7 45.7 %psum.31 = f32[8,1024]{1,0:T(8,128)S(1)} all-reduce(f32[8,1024]{1,0:T(8,128)S(1)} %fusion.56), channel_id=1, replica_groups=mesh['rows'=16,'feat'=16] {'rows'}, use_global_device_ids=true, to_apply=%region_4.4 | all-reduce | flops 8192 | bytes 65536 | tf_op jit(solution)/shard_map/while/body/eval_jaxpr/psum | solution.py:26
  1377.5 7.2 collective-permute-done.1
  1386.7 45.7 %psum.31 = f32[8,1024]{1,0:T(8,128)S(1)} all-reduce(f32[8,1024]{1,0:T(8,128)S(1)} %fusion.56), channel_id=1, replica_groups=mesh['rows'=16,'feat'=16] {'rows'}, use_global_device_ids=true, to_apply=%region_4.4 | all-reduce | flops 8192 | bytes 65536 | tf_op jit(solution)/shard_map/while/body/eval_jaxpr/psum | solution.py:26
  1437.5 7.2 collective-permute-done.1
  1446.6 45.7 %psum.31 = f32[8,1024]{1,0:T(8,128)S(1)} all-reduce(f32[8,1024]{1,0:T(8,128)S(1)} %fusion.56), channel_id=1, replica_groups=mesh['rows'=16,'feat'=16] {'rows'}, use_global_device_ids=true, to_apply=%region_4.4 | all-reduce | flops 8192 | bytes 65536 | tf_op jit(solution)/shard_map/while/body/eval_jaxpr/psum | solution.py:26
  1497.4 7.2 collective-permute-done.1
  1506.6 45.7 %psum.31 = f32[8,1024]{1,0:T(8,128)S(1)} all-reduce(f32[8,1024]{1,0:T(8,128)S(1)} %fusion.56), channel_id=1, replica_groups=mesh['rows'=16,'feat'=16] {'rows'}, use_global_device_ids=true, to_apply=%region_4.4 | all-reduce | flops 8192 | bytes 65536 | tf_op jit(solution)/shard_map/while/body/eval_jaxpr/psum | solution.py:26
  1557.4 7.2 collective-permute-done.1
  1566.6 45.7 %psum.31 = f32[8,1024]{1,0:T(8,128)S(1)} all-reduce(f32[8,1024]{1,0:T(8,128)S(1)} %fusion.56), channel_id=1, replica_groups=mesh['rows'=16,'feat'=16] {'rows'}, use_global_device_ids=true, to_apply=%region_4.4 | all-reduce | flops 8192 | bytes 65536 | tf_op jit(solution)/shard_map/while/body/eval_jaxpr/psum | solution.py:26
  1617.4 7.2 collective-permute-done.1
  1626.6 45.7 %psum.31 = f32[8,1024]{1,0:T(8,128)S(1)} all-reduce(f32[8,1024]{1,0:T(8,128)S(1)} %fusion.56), channel_id=1, replica_groups=mesh['rows'=16,'feat'=16] {'rows'}, use_global_device_ids=true, to_apply=%region_4.4 | all-reduce | flops 8192 | bytes 65536 | tf_op jit(solution)/shard_map/while/body/eval_jaxpr/psum | solution.py:26
  1677.4 7.2 collective-permute-done.1
  1686.6 45.7 %psum.31 = f32[8,1024]{1,0:T(8,128)S(1)} all-reduce(f32[8,1024]{1,0:T(8,128)S(1)} %fusion.56), channel_id=1, replica_groups=mesh['rows'=16,'feat'=16] {'rows'}, use_global_device_ids=true, to_apply=%region_4.4 | all-reduce | flops 8192 | bytes 65536 | tf_op jit(solution)/shard_map/while/body/eval_jaxpr/psum | solution.py:26
  1737.4 7.2 collective-permute-done.1
  1746.6 45.7 %psum.31 = f32[8,1024]{1,0:T(8,128)S(1)} all-reduce(f32[8,1024]{1,0:T(8,128)S(1)} %fusion.56), channel_id=1, replica_groups=mesh['rows'=16,'feat'=16] {'rows'}, use_global_device_ids=true, to_apply=%region_4.4 | all-reduce | flops 8192 | bytes 65536 | tf_op jit(solution)/shard_map/while/body/eval_jaxpr/psum | solution.py:26
  1797.4 7.2 collective-permute-done.1
  1806.6 45.7 %psum.31 = f32[8,1024]{1,0:T(8,128)S(1)} all-reduce(f32[8,1024]{1,0:T(8,128)S(1)} %fusion.56), channel_id=1, replica_groups=mesh['rows'=16,'feat'=16] {'rows'}, use_global_device_ids=true, to_apply=%region_4.4 | all-reduce | flops 8192 | bytes 65536 | tf_op jit(solution)/shard_map/while/body/eval_jaxpr/psum | solution.py:26
  1857.4 7.2 collective-permute-done.1
  1866.6 45.7 %psum.31 = f32[8,1024]{1,0:T(8,128)S(1)} all-reduce(f32[8,1024]{1,0:T(8,128)S(1)} %fusion.56), channel_id=1, replica_groups=mesh['rows'=16,'feat'=16] {'rows'}, use_global_device_ids=true, to_apply=%region_4.4 | all-reduce | flops 8192 | bytes 65536 | tf_op jit(solution)/shard_map/while/body/eval_jaxpr/psum | solution.py:26
  (231 shorter events, 241.7 us)
Async XLA Ops:
  52.6 4.4 copy-start
  57.7 7.3 collective-permute-start
  112.6 4.4 copy-start
  117.7 7.3 collective-permute-start
  172.6 4.4 copy-start
  177.6 7.3 collective-permute-start
  232.6 4.4 copy-start
  237.6 7.3 collective-permute-start
  292.6 4.4 copy-start
  297.6 7.3 collective-permute-start
  352.5 4.4 copy-start
  357.6 7.3 collective-permute-start
  412.5 4.4 copy-start
  417.6 7.3 collective-permute-start
  472.5 4.4 copy-start
  477.6 7.3 collective-permute-start
  532.5 4.4 copy-start
  537.6 7.3 collective-permute-start
  592.5 4.4 copy-start
  597.6 7.3 collective-permute-start
  652.5 4.4 copy-start
  657.6 7.3 collective-permute-start
  712.5 4.4 copy-start
  717.5 7.3 collective-permute-start
  772.5 4.4 copy-start
  777.5 7.3 collective-permute-start
  832.5 4.4 copy-start
  837.5 7.3 collective-permute-start
  892.5 4.4 copy-start
  897.5 7.3 collective-permute-start
  952.4 4.4 copy-start
  957.5 7.3 collective-permute-start
  1012.4 4.4 copy-start.1
  1017.5 7.3 collective-permute-start.1
  1072.4 4.4 copy-start.1
  1077.5 7.3 collective-permute-start.1
  1132.4 4.4 copy-start.1
  1137.5 7.3 collective-permute-start.1
  1192.4 4.4 copy-start.1
  1197.5 7.3 collective-permute-start.1
  1252.4 4.4 copy-start.1
  1257.5 7.3 collective-permute-start.1
  1312.4 4.4 copy-start.1
  1317.4 7.3 collective-permute-start.1
  1372.4 4.4 copy-start.1
  1377.4 7.3 collective-permute-start.1
  1432.4 4.4 copy-start.1
  1437.4 7.3 collective-permute-start.1
  1492.3 4.4 copy-start.1
  1497.4 7.3 collective-permute-start.1
  1552.3 4.4 copy-start.1
  1557.4 7.3 collective-permute-start.1
  1612.3 4.4 copy-start.1
  1617.4 7.3 collective-permute-start.1
  1672.3 4.4 copy-start.1
  1677.4 7.3 collective-permute-start.1
  1732.3 4.4 copy-start.1
  1737.4 7.3 collective-permute-start.1
  1792.3 4.4 copy-start.1
  1797.4 7.3 collective-permute-start.1
  1852.3 4.4 copy-start.1
  1857.3 7.3 collective-permute-start.1
  1912.3 4.4 copy-start.1
  1917.3 7.3 collective-permute-start.1
  (1 other events, 0.8 us)
where the time goes:
time: 1930 us
  blocking collectives  1470 us (76%)
  waiting for transfers between devices  229 us (12%)
  matrix products  225 us (12%)
    psum x32, blocking collectives, refine(): projection = lax.psum(partial_value, 'rows')  1470 us
    ppermute x32, waiting for transfers between devices, passed_along(): return lax.ppermute(block, axis, route)  229 us
    dot_general x32, matrix products, refine(): jnp.dot(projection - ridge_weight * panel_weights, inverse_gram, precisio...  141 us
    dot_general x32, matrix products, refine(): jnp.dot(panel_rows.astype(jnp.bfloat16), features, preferred_element_type...  63.1 us
  transfers between devices with their start and end apart: 32, of which 32 were waited for; matrix products, arithmetic and copies ran while one was open for 0% of the time, Pallas kernels for 0%

commit v1 on v0

--- a/solution.py
+++ b/solution.py
@@ -23,7 +23,8 @@
         partial_value = jnp.dot(
             panel_rows.astype(jnp.bfloat16), features, preferred_element_type=jnp.float32
         )
-        projection = lax.psum(partial_value, "rows")
+        lift_the_orders = lambda obj: jax.lax.all_gather(obj, axis_name="rows").sum(axis=0)
+        projection = lift_the_orders(partial_value)
         increment = jnp.dot(
             projection - ridge_weight * panel_weights, inverse_gram, precision=lax.Precision.HIGHEST
         )

time: 1930 us -> 996 us (0.52)
  blocking collectives: 1470 us -> 532 us
    psum x32 -> x0, blocking collectives: 1470 us -> none  [refine(): projection = lax.psum(partial_value, 'rows')]
    all_gather x0 -> x32, blocking collectives: none -> 532 us  [refine(): jax.lax.all_gather(obj, axis_name='rows').sum(axis=0)]
where the time goes in v1:
time: 996 us; the launch traced here: 993 us
  blocking collectives  532 us (53%)
  waiting for transfers between devices  229 us (23%)
  matrix products  225 us (23%)
    all_gather x32, blocking collectives, refine(): jax.lax.all_gather(obj, axis_name='rows').sum(axis=0)  532 us
    ppermute x32, waiting for transfers between devices, passed_along(): return lax.ppermute(block, axis, route)  229 us
    dot_general x32, matrix products, refine(): jnp.dot(projection - ridge_weight * panel_weights, inverse_gram, precisio...  141 us
    dot_general x32, matrix products, refine(): jnp.dot(panel_rows.astype(jnp.bfloat16), features, preferred_element_type...  63.1 us
    dot_general x32, matrix products, refine(): lax.dot_general(increment.astype(jnp.bfloat16), features, (((1,), (1,)),...  20.6 us
  transfers between devices with their start and end apart: 32, of which 32 were waited for; matrix products, arithmetic and copies ran while one was open for 0% of the time, Pallas kernels for 0%

profile of v1, /device:TPU:0, one launch (start us, length us, event | category | flops | bytes accessed | tf_op | source)
XLA Modules:
  0.0 993.1 jit_solution(2038816865999064477)
XLA Ops:
  1.4 496.6 %while.34 = (s32[]{:T(128)}, f32[8,1024]{1,0:T(8,128)S(1)}, f32[128,1024]{1,0:T(8,128)S(1)}, bf16[1024,1024]{1,0:T(8,128)(2,1)}, s32[]{:T(128)}, /*index=5*/f32[...) while((s32[]{:T(128)}, f32[8,1024]{1,0:T(8,128)S(1)}, ...), condition=%wide.region_2.3_spmd, body=%wide.region_0.2_spmd.sunk | while | flops 134389760 | bytes 18383208 | solution.py:56
  3.4 19.7 %all-gather.4 = f32[128,1024]{1,0:T(8,128)S(1)} all-gather(f32[8,1024]{1,0:T(8,128)S(1)} %fusion.48), channel_id=2, replica_groups=mesh['rows'=16,'feat'=16] {'rows'}, dimensions={0}, use_global_device_ids=true | all-gather | bytes 557056 | tf_op jit(solution)/shard_map/while/body/eval_jaxpr/all_gather | solution.py:26
  37.5 15.7 %all-gather.4 = f32[128,1024]{1,0:T(8,128)S(1)} all-gather(f32[8,1024]{1,0:T(8,128)S(1)} %fusion.48), channel_id=2, replica_groups=mesh['rows'=16,'feat'=16] {'rows'}, dimensions={0}, use_global_device_ids=true | all-gather | bytes 557056 | tf_op jit(solution)/shard_map/while/body/eval_jaxpr/all_gather | solution.py:26
  58.3 7.2 collective-permute-done
  67.5 17.4 %all-gather.4 = f32[128,1024]{1,0:T(8,128)S(1)} all-gather(f32[8,1024]{1,0:T(8,128)S(1)} %fusion.48), channel_id=2, replica_groups=mesh['rows'=16,'feat'=16] {'rows'}, dimensions={0}, use_global_device_ids=true | all-gather | bytes 557056 | tf_op jit(solution)/shard_map/while/body/eval_jaxpr/all_gather | solution.py:26
  90.1 7.2 collective-permute-done
  99.3 15.7 %all-gather.4 = f32[128,1024]{1,0:T(8,128)S(1)} all-gather(f32[8,1024]{1,0:T(8,128)S(1)} %fusion.48), channel_id=2, replica_groups=mesh['rows'=16,'feat'=16] {'rows'}, dimensions={0}, use_global_device_ids=true | all-gather | bytes 557056 | tf_op jit(solution)/shard_map/while/body/eval_jaxpr/all_gather | solution.py:26
  120.1 7.2 collective-permute-done
  129.3 17.4 %all-gather.4 = f32[128,1024]{1,0:T(8,128)S(1)} all-gather(f32[8,1024]{1,0:T(8,128)S(1)} %fusion.48), channel_id=2, replica_groups=mesh['rows'=16,'feat'=16] {'rows'}, dimensions={0}, use_global_device_ids=true | all-gather | bytes 557056 | tf_op jit(solution)/shard_map/while/body/eval_jaxpr/all_gather | solution.py:26
  151.8 7.2 collective-permute-done
  161.0 15.7 %all-gather.4 = f32[128,1024]{1,0:T(8,128)S(1)} all-gather(f32[8,1024]{1,0:T(8,128)S(1)} %fusion.48), channel_id=2, replica_groups=mesh['rows'=16,'feat'=16] {'rows'}, dimensions={0}, use_global_device_ids=true | all-gather | bytes 557056 | tf_op jit(solution)/shard_map/while/body/eval_jaxpr/all_gather | solution.py:26
  181.9 7.2 collective-permute-done
  191.1 17.4 %all-gather.4 = f32[128,1024]{1,0:T(8,128)S(1)} all-gather(f32[8,1024]{1,0:T(8,128)S(1)} %fusion.48), channel_id=2, replica_groups=mesh['rows'=16,'feat'=16] {'rows'}, dimensions={0}, use_global_device_ids=true | all-gather | bytes 557056 | tf_op jit(solution)/shard_map/while/body/eval_jaxpr/all_gather | solution.py:26
  213.6 7.2 collective-permute-done
  222.8 15.7 %all-gather.4 = f32[128,1024]{1,0:T(8,128)S(1)} all-gather(f32[8,1024]{1,0:T(8,128)S(1)} %fusion.48), channel_id=2, replica_groups=mesh['rows'=16,'feat'=16] {'rows'}, dimensions={0}, use_global_device_ids=true | all-gather | bytes 557056 | tf_op jit(solution)/shard_map/while/body/eval_jaxpr/all_gather | solution.py:26
  243.7 7.2 collective-permute-done
  252.9 17.4 %all-gather.4 = f32[128,1024]{1,0:T(8,128)S(1)} all-gather(f32[8,1024]{1,0:T(8,128)S(1)} %fusion.48), channel_id=2, replica_groups=mesh['rows'=16,'feat'=16] {'rows'}, dimensions={0}, use_global_device_ids=true | all-gather | bytes 557056 | tf_op jit(solution)/shard_map/while/body/eval_jaxpr/all_gather | solution.py:26
  275.4 7.2 collective-permute-done
  284.6 15.7 %all-gather.4 = f32[128,1024]{1,0:T(8,128)S(1)} all-gather(f32[8,1024]{1,0:T(8,128)S(1)} %fusion.48), channel_id=2, replica_groups=mesh['rows'=16,'feat'=16] {'rows'}, dimensions={0}, use_global_device_ids=true | all-gather | bytes 557056 | tf_op jit(solution)/shard_map/while/body/eval_jaxpr/all_gather | solution.py:26
  305.5 7.2 collective-permute-done
  314.6 17.4 %all-gather.4 = f32[128,1024]{1,0:T(8,128)S(1)} all-gather(f32[8,1024]{1,0:T(8,128)S(1)} %fusion.48), channel_id=2, replica_groups=mesh['rows'=16,'feat'=16] {'rows'}, dimensions={0}, use_global_device_ids=true | all-gather | bytes 557056 | tf_op jit(solution)/shard_map/while/body/eval_jaxpr/all_gather | solution.py:26
  337.2 7.2 collective-permute-done
  346.4 15.7 %all-gather.4 = f32[128,1024]{1,0:T(8,128)S(1)} all-gather(f32[8,1024]{1,0:T(8,128)S(1)} %fusion.48), channel_id=2, replica_groups=mesh['rows'=16,'feat'=16] {'rows'}, dimensions={0}, use_global_device_ids=true | all-gather | bytes 557056 | tf_op jit(solution)/shard_map/while/body/eval_jaxpr/all_gather | solution.py:26
  367.2 7.2 collective-permute-done
  376.4 17.4 %all-gather.4 = f32[128,1024]{1,0:T(8,128)S(1)} all-gather(f32[8,1024]{1,0:T(8,128)S(1)} %fusion.48), channel_id=2, replica_groups=mesh['rows'=16,'feat'=16] {'rows'}, dimensions={0}, use_global_device_ids=true | all-gather | bytes 557056 | tf_op jit(solution)/shard_map/while/body/eval_jaxpr/all_gather | solution.py:26
  399.0 7.2 collective-permute-done
  408.2 15.7 %all-gather.4 = f32[128,1024]{1,0:T(8,128)S(1)} all-gather(f32[8,1024]{1,0:T(8,128)S(1)} %fusion.48), channel_id=2, replica_groups=mesh['rows'=16,'feat'=16] {'rows'}, dimensions={0}, use_global_device_ids=true | all-gather | bytes 557056 | tf_op jit(solution)/shard_map/while/body/eval_jaxpr/all_gather | solution.py:26
  429.0 7.2 collective-permute-done
  438.2 17.4 %all-gather.4 = f32[128,1024]{1,0:T(8,128)S(1)} all-gather(f32[8,1024]{1,0:T(8,128)S(1)} %fusion.48), channel_id=2, replica_groups=mesh['rows'=16,'feat'=16] {'rows'}, dimensions={0}, use_global_device_ids=true | all-gather | bytes 557056 | tf_op jit(solution)/shard_map/while/body/eval_jaxpr/all_gather | solution.py:26
  460.8 7.2 collective-permute-done
  469.9 15.7 %all-gather.4 = f32[128,1024]{1,0:T(8,128)S(1)} all-gather(f32[8,1024]{1,0:T(8,128)S(1)} %fusion.48), channel_id=2, replica_groups=mesh['rows'=16,'feat'=16] {'rows'}, dimensions={0}, use_global_device_ids=true | all-gather | bytes 557056 | tf_op jit(solution)/shard_map/while/body/eval_jaxpr/all_gather | solution.py:26
  490.8 7.2 collective-permute-done
  498.0 494.3 %while.35 = (s32[]{:T(128)}, f32[8,1024]{1,0:T(8,128)S(1)}, f32[128,1024]{1,0:T(8,128)S(1)}, bf16[1024,1024]{1,0:T(8,128)(2,1)}, s32[]{:T(128)}, /*index=5*/f32[...) while((s32[]{:T(128)}, f32[8,1024]{1,0:T(8,128)S(1)}, ...), condition=%wide.region_5.6_spmd, body=%wide.region_3.5_spmd.sunk | while | flops 134389760 | bytes 18383220 | solution.py:56
  500.0 17.4 %all-gather.5 = f32[128,1024]{1,0:T(8,128)S(1)} all-gather(f32[8,1024]{1,0:T(8,128)S(1)} %fusion.56), channel_id=3, replica_groups=mesh['rows'=16,'feat'=16] {'rows'}, dimensions={0}, use_global_device_ids=true | all-gather | bytes 557056 | tf_op jit(solution)/shard_map/while/body/eval_jaxpr/all_gather | solution.py:26
  522.5 7.2 collective-permute-done.1
  531.7 15.7 %all-gather.5 = f32[128,1024]{1,0:T(8,128)S(1)} all-gather(f32[8,1024]{1,0:T(8,128)S(1)} %fusion.56), channel_id=3, replica_groups=mesh['rows'=16,'feat'=16] {'rows'}, dimensions={0}, use_global_device_ids=true | all-gather | bytes 557056 | tf_op jit(solution)/shard_map/while/body/eval_jaxpr/all_gather | solution.py:26
  552.6 7.2 collective-permute-done.1
  561.8 17.4 %all-gather.5 = f32[128,1024]{1,0:T(8,128)S(1)} all-gather(f32[8,1024]{1,0:T(8,128)S(1)} %fusion.56), channel_id=3, replica_groups=mesh['rows'=16,'feat'=16] {'rows'}, dimensions={0}, use_global_device_ids=true | all-gather | bytes 557056 | tf_op jit(solution)/shard_map/while/body/eval_jaxpr/all_gather | solution.py:26
  584.3 7.2 collective-permute-done.1
  593.5 15.7 %all-gather.5 = f32[128,1024]{1,0:T(8,128)S(1)} all-gather(f32[8,1024]{1,0:T(8,128)S(1)} %fusion.56), channel_id=3, replica_groups=mesh['rows'=16,'feat'=16] {'rows'}, dimensions={0}, use_global_device_ids=true | all-gather | bytes 557056 | tf_op jit(solution)/shard_map/while/body/eval_jaxpr/all_gather | solution.py:26
  614.4 7.2 collective-permute-done.1
  623.6 17.4 %all-gather.5 = f32[128,1024]{1,0:T(8,128)S(1)} all-gather(f32[8,1024]{1,0:T(8,128)S(1)} %fusion.56), channel_id=3, replica_groups=mesh['rows'=16,'feat'=16] {'rows'}, dimensions={0}, use_global_device_ids=true | all-gather | bytes 557056 | tf_op jit(solution)/shard_map/while/body/eval_jaxpr/all_gather | solution.py:26
  646.1 7.2 collective-permute-done.1
  655.3 15.7 %all-gather.5 = f32[128,1024]{1,0:T(8,128)S(1)} all-gather(f32[8,1024]{1,0:T(8,128)S(1)} %fusion.56), channel_id=3, replica_groups=mesh['rows'=16,'feat'=16] {'rows'}, dimensions={0}, use_global_device_ids=true | all-gather | bytes 557056 | tf_op jit(solution)/shard_map/while/body/eval_jaxpr/all_gather | solution.py:26
  676.1 7.2 collective-permute-done.1
  685.3 17.4 %all-gather.5 = f32[128,1024]{1,0:T(8,128)S(1)} all-gather(f32[8,1024]{1,0:T(8,128)S(1)} %fusion.56), channel_id=3, replica_groups=mesh['rows'=16,'feat'=16] {'rows'}, dimensions={0}, use_global_device_ids=true | all-gather | bytes 557056 | tf_op jit(solution)/shard_map/while/body/eval_jaxpr/all_gather | solution.py:26
  707.9 7.2 collective-permute-done.1
  717.1 15.7 %all-gather.5 = f32[128,1024]{1,0:T(8,128)S(1)} all-gather(f32[8,1024]{1,0:T(8,128)S(1)} %fusion.56), channel_id=3, replica_groups=mesh['rows'=16,'feat'=16] {'rows'}, dimensions={0}, use_global_device_ids=true | all-gather | bytes 557056 | tf_op jit(solution)/shard_map/while/body/eval_jaxpr/all_gather | solution.py:26
  737.9 7.2 collective-permute-done.1
  747.1 17.4 %all-gather.5 = f32[128,1024]{1,0:T(8,128)S(1)} all-gather(f32[8,1024]{1,0:T(8,128)S(1)} %fusion.56), channel_id=3, replica_groups=mesh['rows'=16,'feat'=16] {'rows'}, dimensions={0}, use_global_device_ids=true | all-gather | bytes 557056 | tf_op jit(solution)/shard_map/while/body/eval_jaxpr/all_gather | solution.py:26
  769.7 7.2 collective-permute-done.1
  778.9 15.7 %all-gather.5 = f32[128,1024]{1,0:T(8,128)S(1)} all-gather(f32[8,1024]{1,0:T(8,128)S(1)} %fusion.56), channel_id=3, replica_groups=mesh['rows'=16,'feat'=16] {'rows'}, dimensions={0}, use_global_device_ids=true | all-gather | bytes 557056 | tf_op jit(solution)/shard_map/while/body/eval_jaxpr/all_gather | solution.py:26
  799.7 7.2 collective-permute-done.1
  808.9 17.4 %all-gather.5 = f32[128,1024]{1,0:T(8,128)S(1)} all-gather(f32[8,1024]{1,0:T(8,128)S(1)} %fusion.56), channel_id=3, replica_groups=mesh['rows'=16,'feat'=16] {'rows'}, dimensions={0}, use_global_device_ids=true | all-gather | bytes 557056 | tf_op jit(solution)/shard_map/while/body/eval_jaxpr/all_gather | solution.py:26
  831.4 7.2 collective-permute-done.1
  840.6 15.7 %all-gather.5 = f32[128,1024]{1,0:T(8,128)S(1)} all-gather(f32[8,1024]{1,0:T(8,128)S(1)} %fusion.56), channel_id=3, replica_groups=mesh['rows'=16,'feat'=16] {'rows'}, dimensions={0}, use_global_device_ids=true | all-gather | bytes 557056 | tf_op jit(solution)/shard_map/while/body/eval_jaxpr/all_gather | solution.py:26
  861.5 7.2 collective-permute-done.1
  870.7 17.4 %all-gather.5 = f32[128,1024]{1,0:T(8,128)S(1)} all-gather(f32[8,1024]{1,0:T(8,128)S(1)} %fusion.56), channel_id=3, replica_groups=mesh['rows'=16,'feat'=16] {'rows'}, dimensions={0}, use_global_device_ids=true | all-gather | bytes 557056 | tf_op jit(solution)/shard_map/while/body/eval_jaxpr/all_gather | solution.py:26
  893.2 7.2 collective-permute-done.1
  902.4 15.7 %all-gather.5 = f32[128,1024]{1,0:T(8,128)S(1)} all-gather(f32[8,1024]{1,0:T(8,128)S(1)} %fusion.56), channel_id=3, replica_groups=mesh['rows'=16,'feat'=16] {'rows'}, dimensions={0}, use_global_device_ids=true | all-gather | bytes 557056 | tf_op jit(solution)/shard_map/while/body/eval_jaxpr/all_gather | solution.py:26
  923.3 7.2 collective-permute-done.1
  932.5 17.4 %all-gather.5 = f32[128,1024]{1,0:T(8,128)S(1)} all-gather(f32[8,1024]{1,0:T(8,128)S(1)} %fusion.56), channel_id=3, replica_groups=mesh['rows'=16,'feat'=16] {'rows'}, dimensions={0}, use_global_device_ids=true | all-gather | bytes 557056 | tf_op jit(solution)/shard_map/while/body/eval_jaxpr/all_gather | solution.py:26
  955.0 7.2 collective-permute-done.1
  964.2 15.7 %all-gather.5 = f32[128,1024]{1,0:T(8,128)S(1)} all-gather(f32[8,1024]{1,0:T(8,128)S(1)} %fusion.56), channel_id=3, replica_groups=mesh['rows'=16,'feat'=16] {'rows'}, dimensions={0}, use_global_device_ids=true | all-gather | bytes 557056 | tf_op jit(solution)/shard_map/while/body/eval_jaxpr/all_gather | solution.py:26
  (263 shorter events, 243.0 us)
Async XLA Ops:
  23.2 4.4 copy-start
  28.2 7.3 collective-permute-start
  53.2 4.4 copy-start
  58.3 7.3 collective-permute-start
  85.0 4.4 copy-start
  90.0 7.3 collective-permute-start
  115.0 4.4 copy-start
  120.1 7.3 collective-permute-start
  146.7 4.4 copy-start
  151.8 7.3 collective-permute-start
  176.8 4.4 copy-start
  181.9 7.3 collective-permute-start
  208.5 4.4 copy-start
  213.6 7.3 collective-permute-start
  238.6 4.4 copy-start
  243.6 7.3 collective-permute-start
  270.3 4.4 copy-start
  275.4 7.3 collective-permute-start
  300.4 4.4 copy-start
  305.4 7.3 collective-permute-start
  332.1 4.4 copy-start
  337.2 7.3 collective-permute-start
  362.1 4.4 copy-start
  367.2 7.3 collective-permute-start
  393.9 4.4 copy-start
  398.9 7.3 collective-permute-start
  423.9 4.4 copy-start
  429.0 7.3 collective-permute-start
  455.6 4.4 copy-start
  460.7 7.3 collective-permute-start
  485.7 4.4 copy-start
  490.8 7.3 collective-permute-start
  517.4 4.4 copy-start.1
  522.5 7.3 collective-permute-start.1
  547.5 4.4 copy-start.1
  552.6 7.3 collective-permute-start.1
  579.2 4.4 copy-start.1
  584.3 7.3 collective-permute-start.1
  609.3 4.4 copy-start.1
  614.3 7.3 collective-permute-start.1
  641.0 4.4 copy-start.1
  646.1 7.3 collective-permute-start.1
  671.0 4.4 copy-start.1
  676.1 7.3 collective-permute-start.1
  702.8 4.4 copy-start.1
  707.8 7.3 collective-permute-start.1
  732.8 4.4 copy-start.1
  737.9 7.3 collective-permute-start.1
  764.6 4.4 copy-start.1
  769.6 7.3 collective-permute-start.1
  794.6 4.4 copy-start.1
  799.7 7.3 collective-permute-start.1
  826.3 4.4 copy-start.1
  831.4 7.3 collective-permute-start.1
  856.4 4.4 copy-start.1
  861.5 7.3 collective-permute-start.1
  888.1 4.4 copy-start.1
  893.2 7.3 collective-permute-start.1
  918.2 4.4 copy-start.1
  923.2 7.3 collective-permute-start.1
  949.9 4.4 copy-start.1
  955.0 7.3 collective-permute-start.1
  979.9 4.4 copy-start.1
  985.0 7.3 collective-permute-start.1
  (1 other events, 0.8 us)
